TPU v7x, 32 devices: a whole 2x2x4 slice. The times are simulated.
32 devices in a mesh: dp: 4 (over y, x), mp: 8 (over z, core).
Axes of the slice: x: 2, y: 2, z: 4, core: 2. Of those that a mesh axis runs over, the one named last changes fastest.
Arguments:
- grads: bfloat16 [3, 8192, 28672], P(None, 'dp', 'mp'), may hold values from -8 to 8
- sketch: bfloat16 [28672, 256], P('mp'), may hold values from -0.03125 to 0.03125
- old_proj: bfloat16 [3, 8192, 256], P(None, 'dp'), may hold values from -0.0625 to 0.0625
- first_moment: float32 [3, 256, 28672], P(None, 'dp', 'mp'), may hold values from -12 to 12
- second_moment: float32 [3, 256, 28672], P(None, 'dp', 'mp'), may hold values from 0.25 to 4
- refresh_list: int32 [1], replicated, may hold values from 0 to 2
Outputs:
- new_first: float32 [3, 256, 28672], P(None, 'dp', 'mp')
- new_second: float32 [3, 256, 28672], P(None, 'dp', 'mp')
- direction: bfloat16 [3, 256, 28672], P(None, 'dp', 'mp')
All inputs are finite; a program needn't handle non-finite values.
Results may differ from a plain program's by a relative error of at most 0.0029.
Values sent between devices are 32-bit elements; how exact they have to be, the bound alone decides.
No kernel may reach another device: no remote copies, remote signals or barrier semaphores. Data moves between devices by JAX's collectives and lax.ppermute only.
A program may use at most 192 MiB of HBM per device.

v0:
```python
import jax
import jax.numpy as jnp
from jax import lax
from jax.sharding import PartitionSpec as P

first_decay = 0.9
second_decay = 0.95
epsilon = 1e-08
highest = lax.Precision.HIGHEST


def row_product(left, right):
    return lax.dot_general(
        left, right, (((0,), (0,)), ((), ())), precision=highest, preferred_element_type=jnp.float32
    )


def local(grads, sketch, old_proj, first_moment, second_moment, refresh_list):
    chosen = refresh_list[0]
    matrix_count = grads.shape[0]
    rank_rows = first_moment.shape[1]
    rank_total = sketch.shape[1]
    columns_total = sketch.shape[0] * lax.axis_size("mp")
    target = lax.dynamic_index_in_dim(grads, chosen, 0, keepdims=False)
    prior_proj = lax.dynamic_index_in_dim(old_proj, chosen, 0, keepdims=False).astype(jnp.float32)
    sketch_part = jnp.dot(target, sketch, preferred_element_type=jnp.float32)
    sketched = (lax.psum(sketch_part, "mp") / rank_total).astype(jnp.bfloat16)
    backward_part = lax.dot_general(
        target, sketched, (((0,), (0,)), ((), ())), preferred_element_type=jnp.float32
    )
    backward = (lax.psum(backward_part, "dp") / columns_total).astype(jnp.bfloat16)
    range_panel = lax.psum(jnp.dot(target, backward, preferred_element_type=jnp.float32), "mp")
    gram_part = row_product(range_panel, range_panel)
    gram_full = lax.psum(gram_part, "dp")
    factor = jnp.linalg.cholesky(gram_full)
    new_basis = jax.scipy.linalg.solve_triangular(factor, range_panel.T, lower=True).T
    turning = lax.psum(row_product(new_basis, prior_proj), "dp")
    picks = lax.broadcasted_iota(jnp.int32, (matrix_count, 1, 1), 0) == chosen
    projectors = jnp.where(picks, new_basis.astype(jnp.bfloat16)[None], old_proj)
    projected = jnp.transpose(
        lax.psum_scatter(
            jnp.einsum("kdr,kdc->rkc", projectors, grads, preferred_element_type=jnp.float32),
            "dp",
            scatter_dimension=0,
            tiled=True,
        ),
        (1, 0, 2),
    )
    first_own = lax.dynamic_index_in_dim(first_moment, chosen, 0, keepdims=False)
    second_own = lax.dynamic_index_in_dim(second_moment, chosen, 0, keepdims=False)
    own_start = lax.axis_index("dp") * rank_rows
    first_all, second_all = (
        lax.all_gather(first_own, "dp", axis=0, tiled=True),
        lax.all_gather(second_own, "dp", axis=0, tiled=True),
    )
    own_turning = lax.dynamic_slice_in_dim(turning, own_start, rank_rows, 0)
    turned_first = jnp.dot(own_turning, first_all, precision=highest)
    turned_second = jnp.dot(own_turning * own_turning, second_all, precision=highest)
    moved_first = jnp.where(picks, turned_first[None], first_moment)
    moved_second = jnp.where(picks, turned_second[None], second_moment)
    updated_first = first_decay * moved_first + (1.0 - first_decay) * projected
    updated_second = second_decay * moved_second + (1.0 - second_decay) * projected * projected
    direction = (updated_first / (jnp.sqrt(updated_second) + epsilon)).astype(jnp.bfloat16)
    return (updated_first, updated_second, direction)


def solution(mesh):
    placed = (
        P(None, "dp", "mp"),
        P("mp", None),
        P(None, "dp", None),
        P(None, "dp", "mp"),
        P(None, "dp", "mp"),
        P(),
    )
    return jax.shard_map(
        local,
        mesh=mesh,
        in_specs=placed,
        out_specs=(P(None, "dp", "mp"), P(None, "dp", "mp"), P(None, "dp", "mp")),
        check_vma=False,
    )
```

profile of v0, /device:TPU:0, one launch (start us, length us, event | category | flops | bytes accessed | tf_op | source)
XLA Modules:
  0.0 609.4 jit_solution(3067259670049275815)
XLA Ops:
  8.7 8.6 %fusion.4 = f32[2048,256]{1,0:T(8,128)} fusion(bf16[3584,256]{1,0:T(8,128)(2,1)S(1)} %copy-done, bf16[3,2048,3584]{2,1,0:T(8,128)(2,1)} %param.6, s32[]{:T(128)S(6)} %select_n.27), kind=kOutput, calls=%fused_computation.6 | convolution fusion | flops 3758096384 | bytes 18612228 | tf_op jit(solution)/shard_map/dot_general | solution.py:26
  17.3 68.0 %all-reduce.7.cloned.1.call-done = f32[2048,256]{1,0:T(8,128)} async-done(((f32[2048,256]{1,0:T(8,128)}), f32[2048,256]{1,0:T(8,128)}) %all-reduce.7.cloned.1.call-update) | async-done | bytes 2097168 | tf_op jit(solution)/shard_map/psum | solution.py:27
  85.3 11.6 %fusion.2 = f32[3584,256]{1,0:T(8,128)} fusion(bf16[3,2048,3584]{2,1,0:T(8,128)(2,1)} %param.6, s32[]{:T(128)S(6)} %select_n.27, f32[2048,256]{1,0:T(8,128)} %all-reduce.7.cloned.1.call-done), kind=kOutput, calls=%fused_computation.4 | convolution fusion | flops 3759144960 | bytes 20447236 | tf_op jit(solution)/shard_map/dot_general | solution.py:28
  97.0 95.4 %all-reduce.9.cloned.1.call-done = f32[3584,256]{1,0:T(8,128)} async-done(((f32[3584,256]{1,0:T(8,128)}), f32[3584,256]{1,0:T(8,128)}) %all-reduce.9.cloned.1.call-update) | async-done | bytes 3670032 | tf_op jit(solution)/shard_map/psum | solution.py:31
  192.4 11.5 %fusion = f32[2048,256]{1,0:T(8,128)} fusion(bf16[3,2048,3584]{2,1,0:T(8,128)(2,1)} %param.6, s32[]{:T(128)S(6)} %select_n.27, f32[3584,256]{1,0:T(8,128)} %all-reduce.9.cloned.1.call-done), kind=kOutput, calls=%fused_computation.2 | convolution fusion | flops 3759931392 | bytes 20447236 | tf_op jit(solution)/shard_map/dot_general | solution.py:32
  204.4 64.7 %all-reduce.11.cloned.1.call-done = f32[2048,256]{1,0:T(8,128)} async-done(((f32[2048,256]{1,0:T(8,128)}), f32[2048,256]{1,0:T(8,128)}) %all-reduce.11.cloned.1.call-update) | async-done | bytes 2097168 | tf_op jit(solution)/shard_map/psum | solution.py:32
  269.2 6.4 %fusion.48 = f32[256,256]{0,1:T(8,128)} fusion(f32[2048,256]{1,0:T(8,128)} %all-reduce.11.cloned.1.call-done), kind=kOutput, calls=%fused_computation.75 | convolution fusion | flops 1610612736 | bytes 2359296 | tf_op jit(solution)/shard_map/dot_general | solution.py:13
  275.6 2.2 constant_dynamic-slice_fusion.1
  277.9 40.5 %all-reduce.13.cloned.1.call-done = f32[256,256]{0,1:T(8,128)} async-done(((f32[256,256]{0,1:T(8,128)}), f32[256,256]{0,1:T(8,128)}) %all-reduce.13.cloned.1.call-update) | async-done | bytes 262160 | tf_op jit(solution)/shard_map/psum | solution.py:34
  318.4 1.1 copy.10
  319.5 1.0 fusion.27
  320.5 11.7 %cholesky.50 = f32[128,128]{1,0:T(8,128)S(1)} custom-call(f32[128,128]{1,0:T(8,128)S(1)} %cholesky.118), custom_call_target="Cholesky" | custom-call | tf_op jit(solution)/shard_map/jit(cholesky)/cholesky | solution.py:35
  332.2 9.8 %custom-call.15 = f32[1,128,128]{1,2,0:T(8,128)S(1)} custom-call(f32[1,128,128]{2,1,0:T(8,128)S(1)} %get-tuple-element.27), custom_call_target="InvertDiagBlocksLowerTriangular" | custom-call | tf_op jit(solution)/shard_map/jit(cholesky)/cholesky | solution.py:35
  342.5 11.7 %cholesky.105 = f32[128,128]{1,0:T(8,128)S(1)} custom-call(f32[128,128]{1,0:T(8,128)S(1)} %convolution_subtract_fusion.1), custom_call_target="Cholesky" | custom-call | tf_op jit(solution)/shard_map/jit(cholesky)/cholesky | solution.py:35
  356.5 4.2 while.1
  357.2 1.4 bitcast_dynamic-update-slice_fusion.2
  359.3 1.4 bitcast_dynamic-update-slice_fusion.2
  360.7 19.7 %custom-call.16 = f32[2,128,128]{1,2,0:T(8,128)S(1)} custom-call(f32[2,128,128]{2,1,0:T(8,128)S(1)} %get-tuple-element.10), custom_call_target="InvertDiagBlocksLowerTriangular" | custom-call | tf_op jit(solution)/shard_map/jit(_solve_triangular)/triangular_solve | solution.py:36
  380.4 2.3 fusion.22
  382.7 3.0 convolution_subtract_fusion
  385.7 1.1 fusion.29
  386.8 3.0 fusion.19
  389.9 2.2 constant_dynamic-slice_fusion.2
  392.2 1.1 fusion.21
  393.3 1.7 copy.11
  395.0 24.7 %convolution_bitcast_fusion = f32[256,3,3584]{2,0,1:T(8,128)} fusion(bf16[3,2048,3584]{2,1,0:T(8,128)(2,1)} %param.6, bf16[3,2048,256]{2,1,0:T(8,128)(2,1)} %param.8, pred[3]{0:T(512)(128)(4,1)S(1)} %iota_compare_fusion.3, bf16[2048,256]{1,0:T(8,128)(2,1)S(1)} %copy.11), kind=kOutput, calls=%fused_computation.11 | convolution fusion | flops 11275862016 | bytes 59244548 | tf_op jit(solution)/shard_map/kdr,kdc->rkc/dot_general | solution.py:42
  419.8 13.3 %all-reduce.15.cloned.1.call-done = f32[256,256]{1,0:T(8,128)} async-done(((f32[256,256]{1,0:T(8,128)}), f32[256,256]{1,0:T(8,128)}) %all-reduce.15.cloned.1.call-update) | async-done | bytes 262160 | tf_op jit(solution)/shard_map/psum | solution.py:37
  433.0 4.4 fusion.9
  437.4 46.3 %all-gather.5.cloned.1.call-done = f32[1,256,3584]{2,1,0:T(8,128)} async-done(((f32[1,64,3584]{2,1,0:T(8,128)}), f32[1,256,3584]{2,1,0:T(8,128)}) %all-gather.5.cloned.1.call-update) | async-done | bytes 3670032 | tf_op jit(solution)/shard_map/all_gather | solution.py:53
  483.7 5.3 fusion.11
  489.0 105.6 %reduce-scatter.2.cloned.1.call-done = f32[64,3,3584]{2,0,1:T(8,128)} async-done(((f32[256,3,3584]{2,0,1:T(8,128)}), f32[64,3,3584]{2,0,1:T(8,128)}) %reduce-scatter.2.cloned.1.call-update) | async-done | bytes 2752528 | tf_op jit(solution)/shard_map/reduce_scatter | solution.py:41
  594.6 7.8 %divide_convert_fusion = (bf16[3,64,3584]{2,1,0:T(8,128)(2,1)}, f32[3,64,3584]{2,1,0:T(8,128)}, f32[3,64,3584]{2,1,0:T(8,128)}) fusion(f32[64,3,3584]{2,0,1:T(8,128)} %reduce-scatter.2.cloned.1.call-done, f32[3,64,3584]{2,1,0:T(8,128)} %param.10, f32[64,3584]{1,0:T(8,128)S(1)} %fusion.9, pred[3]{0:T(512)(128)(4,1)S(1)} %iota_compare_fusion.3, ...), kind=kLoop, calls=%fused_computation.23 | loop fusion | flops 8257536 | bytes 16973828 | tf_op jit(solution)/shard_map/convert_element_type | solution.py:63
  (37 shorter events, 4.2 us)
Async XLA Ops:
  7.2 1.5 copy-start
  7.2 78.1 %all-reduce.7.cloned.1.call-start = ((), (), s32[]{:S(2)}) async-start(), calls=%async_computation.1 | async-start | bytes 4194304 | tf_op jit(solution)/shard_map/psum | solution.py:27
  17.3 175.1 %all-reduce.9.cloned.1.call-start = ((), (), s32[]{:S(2)}) async-start(), calls=%async_computation.2 | async-start | bytes 7340032 | tf_op jit(solution)/shard_map/psum | solution.py:31
  96.9 172.2 %all-reduce.11.cloned.1.call-start = ((), (), s32[]{:S(2)}) async-start(), calls=%async_computation.3 | async-start | bytes 4194304 | tf_op jit(solution)/shard_map/psum | solution.py:32
  203.9 114.4 %all-reduce.13.cloned.1.call-start = ((), (), s32[]{:S(2)}) async-start(), calls=%async_computation.4 | async-start | bytes 524288 | tf_op jit(solution)/shard_map/psum | solution.py:34
  275.6 144.2 %all-gather.7.cloned.1.call-start = ((), (), s32[]{:S(2)}) async-start(), calls=%async_computation.8 | async-start | bytes 4587520 | tf_op jit(solution)/shard_map/all_gather | solution.py:54
  277.8 155.2 %all-reduce.15.cloned.1.call-start = ((), (), s32[]{:S(2)}) async-start(), calls=%async_computation.5 | async-start | bytes 524288 | tf_op jit(solution)/shard_map/psum | solution.py:37
  389.9 93.8 %all-gather.5.cloned.1.call-start = ((), (), s32[]{:S(2)}) async-start(), calls=%async_computation.7 | async-start | bytes 4587520 | tf_op jit(solution)/shard_map/all_gather | solution.py:53
  392.1 202.5 %reduce-scatter.2.cloned.1.call-start = ((), (), s32[]{:S(2)}) async-start(), calls=%async_computation.6 | async-start | bytes 13762560 | tf_op jit(solution)/shard_map/reduce_scatter | solution.py:41
  594.6 7.8 %copy-start.1 = (bf16[3584,256]{1,0:T(8,128)(2,1)S(1)}, bf16[3584,256]{1,0:T(8,128)(2,1)}, u32[]{:S(2)}) copy-start(bf16[3584,256]{1,0:T(8,128)(2,1)} %param.7) | copy-start | bytes 5505028
Sparse Core Ops, SparseCore 0:
  17.4 67.8 all-reduce.6
  97.0 95.2 all-reduce.8
  204.1 65.0 all-reduce.10
  275.7 42.6 all-reduce.12
  320.6 48.3 all-gather.6
  390.0 43.0 all-reduce.14
  435.5 48.1 all-gather.4
  486.8 107.7 reduce-scatter.1
where the time goes:
time: 617 us; the launch traced here: 609 us
  waiting for transfers between devices  434 us (70%)
  matrix products  82.4 us (13%)
  other arithmetic  63.6 us (10%)
  between operations  16.6 us (3%)
  local copies, waits for them, and re-layouts  11.9 us (2%)
    reduce_scatter x1, waiting for transfers between devices, local(): lax.psum_scatter(jnp.einsum('kdr,kdc->rkc', projectors, grads, preferred_...  106 us
    psum x1, waiting for transfers between devices, local(): lax.psum(backward_part, 'dp') / columns_total  95.4 us
    psum x1, waiting for transfers between devices, local(): sketched = (lax.psum(sketch_part, 'mp') / rank_total).astype(jnp.bfloat16)  68 us
    psum x1, waiting for transfers between devices, local(): lax.psum(jnp.dot(target, backward, preferred_element_type=jnp.float32), '...  64.7 us
    all_gather x1, waiting for transfers between devices, local(): lax.all_gather(first_own, 'dp', axis=0, tiled=True)  46.3 us
    psum x1, waiting for transfers between devices, local(): gram_full = lax.psum(gram_part, 'dp')  40.5 us
    another operation x6, other arithmetic, local(): factor = jnp.linalg.cholesky(gram_full)  34 us
    dot_general x1, matrix products, local(): jnp.einsum('kdr,kdc->rkc', projectors, grads, preferred_element_type=jnp....  24.7 us
  transfers between devices with their start and end apart: 8, of which 7 were waited for; matrix products, arithmetic and copies ran while one was open for 18% of the time, Pallas kernels for 0%

commit v1 on v0

--- a/solution.py
+++ b/solution.py
@@ -7,6 +7,14 @@
 second_decay = 0.95
 epsilon = 1e-08
 highest = lax.Precision.HIGHEST
+
+
+def _switch_field(payload):
+    far_arr = payload
+    world = lax.axis_size("dp")
+    for k in [[(it, it ^ kk) for it in range(world)] for kk in (1, 2, 4, 8, 16) if kk < world]:
+        far_arr = far_arr + lax.ppermute(far_arr, axis_name="dp", perm=k)
+    return far_arr
 
 
 def row_product(left, right):
@@ -31,7 +39,7 @@
     backward = (lax.psum(backward_part, "dp") / columns_total).astype(jnp.bfloat16)
     range_panel = lax.psum(jnp.dot(target, backward, preferred_element_type=jnp.float32), "mp")
     gram_part = row_product(range_panel, range_panel)
-    gram_full = lax.psum(gram_part, "dp")
+    gram_full = _switch_field(gram_part)
     factor = jnp.linalg.cholesky(gram_full)
     new_basis = jax.scipy.linalg.solve_triangular(factor, range_panel.T, lower=True).T
     turning = lax.psum(row_product(new_basis, prior_proj), "dp")

time: 617 us -> 591 us (0.958)
  waiting for transfers between devices: 434 us -> 408 us
    psum x1 -> x0, waiting for transfers between devices: 40.5 us -> none  [local(): gram_full = lax.psum(gram_part, 'dp')]
    ppermute x0 -> x2, waiting for transfers between devices: none -> 18.7 us  [_switch_field(): far_arr = far_arr + lax.ppermute(far_arr, axis_name='dp', perm=k)]
  transfers between devices with their start and end apart: 8 -> 9, of which waited for: 7 -> 8; matrix products, arithmetic and copies ran while one was open for 18% -> 20% of each run, Pallas kernels for 0% -> 0%
where the time goes in v1:
time: 591 us; the launch traced here: 583 us
  waiting for transfers between devices  408 us (69%)
  matrix products  81.5 us (14%)
  other arithmetic  62.9 us (11%)
  between operations  16.5 us (3%)
  local copies, waits for them, and re-layouts  10.6 us (2%)
    reduce_scatter x1, waiting for transfers between devices, local(): lax.psum_scatter(jnp.einsum('kdr,kdc->rkc', projectors, grads, preferred_...  106 us
    psum x1, waiting for transfers between devices, local(): lax.psum(backward_part, 'dp') / columns_total  95.4 us
    psum x1, waiting for transfers between devices, local(): sketched = (lax.psum(sketch_part, 'mp') / rank_total).astype(jnp.bfloat16)  68 us
    psum x1, waiting for transfers between devices, local(): lax.psum(jnp.dot(target, backward, preferred_element_type=jnp.float32), '...  62.5 us
    all_gather x1, waiting for transfers between devices, local(): lax.all_gather(first_own, 'dp', axis=0, tiled=True)  46.1 us
    another operation x6, other arithmetic, local(): factor = jnp.linalg.cholesky(gram_full)  34.2 us
    dot_general x1, matrix products, local(): jnp.einsum('kdr,kdc->rkc', projectors, grads, preferred_element_type=jnp....  24.6 us
    another operation x3, other arithmetic, local(): jax.scipy.linalg.solve_triangular(factor, range_panel.T, lower=True)  19.7 us
  transfers between devices with their start and end apart: 9, of which 8 were waited for; matrix products, arithmetic and copies ran while one was open for 20% of the time, Pallas kernels for 0%

profile of v1, /device:TPU:0, one launch (start us, length us, event | category | flops | bytes accessed | tf_op | source)
XLA Modules:
  0.0 583.2 jit_solution(1167710816651924543)
XLA Ops:
  8.7 8.6 %fusion.4 = f32[2048,256]{1,0:T(8,128)} fusion(bf16[3584,256]{1,0:T(8,128)(2,1)S(1)} %copy-done, bf16[3,2048,3584]{2,1,0:T(8,128)(2,1)} %param.6, s32[]{:T(128)S(6)} %select_n.27), kind=kOutput, calls=%fused_computation.6 | convolution fusion | flops 3758096384 | bytes 18612228 | tf_op jit(solution)/shard_map/dot_general | solution.py:34
  17.3 68.0 %all-reduce.6.cloned.1.call-done = f32[2048,256]{1,0:T(8,128)} async-done(((f32[2048,256]{1,0:T(8,128)}), f32[2048,256]{1,0:T(8,128)}) %all-reduce.6.cloned.1.call-update) | async-done | bytes 2097168 | tf_op jit(solution)/shard_map/psum | solution.py:35
  85.3 11.6 %fusion.2 = f32[3584,256]{1,0:T(8,128)} fusion(bf16[3,2048,3584]{2,1,0:T(8,128)(2,1)} %param.6, s32[]{:T(128)S(6)} %select_n.27, f32[2048,256]{1,0:T(8,128)} %all-reduce.6.cloned.1.call-done), kind=kOutput, calls=%fused_computation.4 | convolution fusion | flops 3759144960 | bytes 20447236 | tf_op jit(solution)/shard_map/dot_general | solution.py:36
  97.0 95.4 %all-reduce.8.cloned.1.call-done = f32[3584,256]{1,0:T(8,128)} async-done(((f32[3584,256]{1,0:T(8,128)}), f32[3584,256]{1,0:T(8,128)}) %all-reduce.8.cloned.1.call-update) | async-done | bytes 3670032 | tf_op jit(solution)/shard_map/psum | solution.py:39
  192.4 11.5 %fusion = f32[2048,256]{1,0:T(8,128)} fusion(bf16[3,2048,3584]{2,1,0:T(8,128)(2,1)} %param.6, s32[]{:T(128)S(6)} %select_n.27, f32[3584,256]{1,0:T(8,128)} %all-reduce.8.cloned.1.call-done), kind=kOutput, calls=%fused_computation.2 | convolution fusion | flops 3759931392 | bytes 20447236 | tf_op jit(solution)/shard_map/dot_general | solution.py:40
  204.0 2.2 constant_dynamic-slice_fusion.1
  206.7 62.5 %all-reduce.10.cloned.1.call-done = f32[2048,256]{1,0:T(8,128)} async-done(((f32[2048,256]{1,0:T(8,128)}), f32[2048,256]{1,0:T(8,128)}) %all-reduce.10.cloned.1.call-update) | async-done | bytes 2097168 | tf_op jit(solution)/shard_map/psum | solution.py:40
  269.2 5.7 fusion.48
  274.9 1.5 collective-permute-start
  276.4 6.6 %collective-permute-done = f32[256,256]{0,1:T(8,128)S(1)} collective-permute-done((f32[256,256]{0,1:T(8,128)S(1)}, f32[256,256]{0,1:T(8,128)S(1)}, u32[]{:S(2)}, u32[]{:S(2)}) %collective-permute-start) | collective-permute-done | bytes 262176 | tf_op jit(solution)/shard_map/ppermute | solution.py:16
  284.0 12.1 %collective-permute-done.1 = f32[256,256]{0,1:T(8,128)S(1)} collective-permute-done((f32[256,256]{0,1:T(8,128)S(1)}, f32[256,256]{0,1:T(8,128)S(1)}, u32[]{:S(2)}, u32[]{:S(2)}) %collective-permute-start.1) | collective-permute-done | bytes 262176 | tf_op jit(solution)/shard_map/ppermute | solution.py:16
  296.3 11.7 %cholesky.50 = f32[128,128]{1,0:T(8,128)S(1)} custom-call(f32[128,128]{1,0:T(8,128)S(1)} %cholesky.118), custom_call_target="Cholesky" | custom-call | tf_op jit(solution)/shard_map/jit(cholesky)/cholesky | solution.py:43
  308.1 9.8 %custom-call.15 = f32[1,128,128]{1,2,0:T(8,128)S(1)} custom-call(f32[1,128,128]{2,1,0:T(8,128)S(1)} %get-tuple-element.27), custom_call_target="InvertDiagBlocksLowerTriangular" | custom-call | tf_op jit(solution)/shard_map/jit(cholesky)/cholesky | solution.py:43
  318.4 11.9 %cholesky.105 = f32[128,128]{1,0:T(8,128)S(1)} custom-call(f32[128,128]{1,0:T(8,128)S(1)} %slice_subtract_fusion), custom_call_target="Cholesky" | custom-call | tf_op jit(solution)/shard_map/jit(cholesky)/cholesky | solution.py:43
  332.4 3.9 while.1
  333.0 1.3 bitcast_dynamic-update-slice_fusion.2
  334.9 1.3 bitcast_dynamic-update-slice_fusion.2
  336.2 19.7 %custom-call.16 = f32[2,128,128]{1,2,0:T(8,128)S(1)} custom-call(f32[2,128,128]{2,1,0:T(8,128)S(1)} %get-tuple-element.10), custom_call_target="InvertDiagBlocksLowerTriangular" | custom-call | tf_op jit(solution)/shard_map/jit(_solve_triangular)/triangular_solve | solution.py:44
  355.9 2.3 fusion.22
  358.2 3.0 convolution_subtract_fusion
  361.3 1.1 fusion.29
  362.3 3.0 fusion.19
  365.4 2.2 constant_dynamic-slice_fusion.2
  367.9 1.1 fusion.21
  369.0 1.5 copy.12
  370.5 24.6 %convolution_bitcast_fusion = f32[256,3,3584]{2,0,1:T(8,128)} fusion(bf16[3,2048,3584]{2,1,0:T(8,128)(2,1)} %param.6, bf16[3,2048,256]{2,1,0:T(8,128)(2,1)} %param.8, pred[3]{0:T(512)(128)(4,1)S(1)} %iota_compare_fusion.3, bf16[2048,256]{1,0:T(8,128)(2,1)S(1)} %copy.12), kind=kOutput, calls=%fused_computation.11 | convolution fusion | flops 11275862016 | bytes 59244548 | tf_op jit(solution)/shard_map/kdr,kdc->rkc/dot_general | solution.py:50
  395.2 11.8 %all-reduce.12.cloned.1.call-done = f32[256,256]{1,0:T(8,128)} async-done(((f32[256,256]{1,0:T(8,128)}), f32[256,256]{1,0:T(8,128)}) %all-reduce.12.cloned.1.call-update) | async-done | bytes 262160 | tf_op jit(solution)/shard_map/psum | solution.py:45
  406.9 4.4 fusion.9
  411.3 46.1 %all-gather.5.cloned.1.call-done = f32[1,256,3584]{2,1,0:T(8,128)} async-done(((f32[1,64,3584]{2,1,0:T(8,128)}), f32[1,256,3584]{2,1,0:T(8,128)}) %all-gather.5.cloned.1.call-update) | async-done | bytes 3670032 | tf_op jit(solution)/shard_map/all_gather | solution.py:61
  457.5 5.3 fusion.11
  462.8 105.6 %reduce-scatter.2.cloned.1.call-done = f32[64,3,3584]{2,0,1:T(8,128)} async-done(((f32[256,3,3584]{2,0,1:T(8,128)}), f32[64,3,3584]{2,0,1:T(8,128)}) %reduce-scatter.2.cloned.1.call-update) | async-done | bytes 2752528 | tf_op jit(solution)/shard_map/reduce_scatter | solution.py:49
  568.4 7.8 %divide_convert_fusion = (bf16[3,64,3584]{2,1,0:T(8,128)(2,1)}, f32[3,64,3584]{2,1,0:T(8,128)}, f32[3,64,3584]{2,1,0:T(8,128)}) fusion(f32[64,3,3584]{2,0,1:T(8,128)} %reduce-scatter.2.cloned.1.call-done, f32[3,64,3584]{2,1,0:T(8,128)} %param.10, f32[64,3584]{1,0:T(8,128)S(1)} %fusion.9, pred[3]{0:T(512)(128)(4,1)S(1)} %iota_compare_fusion.3, ...), kind=kLoop, calls=%fused_computation.23 | loop fusion | flops 8257536 | bytes 16973828 | tf_op jit(solution)/shard_map/convert_element_type | solution.py:71
  (40 shorter events, 5.6 us)
Async XLA Ops:
  7.2 1.5 copy-start
  7.2 78.1 %all-reduce.6.cloned.1.call-start = ((), (), s32[]{:S(2)}) async-start(), calls=%async_computation.1 | async-start | bytes 4194304 | tf_op jit(solution)/shard_map/psum | solution.py:35
  17.3 175.1 %all-reduce.8.cloned.1.call-start = ((), (), s32[]{:S(2)}) async-start(), calls=%async_computation.2 | async-start | bytes 7340032 | tf_op jit(solution)/shard_map/psum | solution.py:39
  96.9 172.2 %all-reduce.10.cloned.1.call-start = ((), (), s32[]{:S(2)}) async-start(), calls=%async_computation.3 | async-start | bytes 4194304 | tf_op jit(solution)/shard_map/psum | solution.py:40
  203.9 191.2 %all-gather.7.cloned.1.call-start = ((), (), s32[]{:S(2)}) async-start(), calls=%async_computation.7 | async-start | bytes 4587520 | tf_op jit(solution)/shard_map/all_gather | solution.py:62
  206.2 200.8 %all-reduce.12.cloned.1.call-start = ((), (), s32[]{:S(2)}) async-start(), calls=%async_computation.4 | async-start | bytes 524288 | tf_op jit(solution)/shard_map/psum | solution.py:45
  274.9 8.1 %collective-permute-start = (f32[256,256]{0,1:T(8,128)S(1)}, f32[256,256]{0,1:T(8,128)S(1)}, u32[]{:S(2)}, u32[]{:S(2)}) collective-permute-start(f32[256,256]{0,1:T(8,128)S(1)} %fusion.48), channel_id=1, source_target_pairs={{0,8},{8,0},{16,24},{24,16},{1,9},{9,1},{17,25},{25,17},{2,10},{10... | collective-permute-start | bytes 786440 | tf_op jit(solution)/shard_map/ppermute | solution.py:16
  283.0 13.1 %collective-permute-start.1 = (f32[256,256]{0,1:T(8,128)S(1)}, f32[256,256]{0,1:T(8,128)S(1)}, u32[]{:S(2)}, u32[]{:S(2)}) collective-permute-start(f32[256,256]{0,1:T(8,128)S(1)} %add.64), channel_id=1, source_target_pairs={{0,16},{8,24},{16,0},{24,8},{1,17},{9,25},{17,1},{25,9},{2,18},{10... | collective-permute-start | bytes 786440 | tf_op jit(solution)/shard_map/ppermute | solution.py:16
  365.4 92.1 %all-gather.5.cloned.1.call-start = ((), (), s32[]{:S(2)}) async-start(), calls=%async_computation.6 | async-start | bytes 4587520 | tf_op jit(solution)/shard_map/all_gather | solution.py:61
  367.6 200.7 %reduce-scatter.2.cloned.1.call-start = ((), (), s32[]{:S(2)}) async-start(), calls=%async_computation.5 | async-start | bytes 13762560 | tf_op jit(solution)/shard_map/reduce_scatter | solution.py:49
  568.4 7.8 %copy-start.1 = (bf16[3584,256]{1,0:T(8,128)(2,1)S(1)}, bf16[3584,256]{1,0:T(8,128)(2,1)}, u32[]{:S(2)}) copy-start(bf16[3584,256]{1,0:T(8,128)(2,1)} %param.7) | copy-start | bytes 5505028
Sparse Core Ops, SparseCore 0:
  17.4 67.8 all-reduce.5
  97.1 95.2 all-reduce.7
  204.1 65.0 all-reduce.9
  271.5 52.0 all-gather.6
  365.5 41.3 all-reduce.11
  409.2 48.1 all-gather.4
  460.6 107.7 reduce-scatter.1
